TPU v7x, 32 devices: a whole 2x2x4 slice. The times are simulated.
32 devices in a mesh: seq: 8 (over z, x), head: 4 (over y, core).
Axes of the slice: x: 2, y: 2, z: 4, core: 2. Of those that a mesh axis runs over, the one named last changes fastest.
Arguments:
- queries: bfloat16 [2, 8, 14336], P(None, 'seq', 'head'), may hold values from -150 to 150
- new_keys: bfloat16 [2, 8, 14336], P(None, 'seq', 'head'), may hold values from -6 to 6
- new_values: bfloat16 [2, 8, 14336], P(None, 'seq', 'head'), may hold values from -6 to 6
- cache_keys: bfloat16 [8192, 14336], P('seq', 'head'), may hold values from -6 to 6
- cache_values: bfloat16 [8192, 14336], P('seq', 'head'), may hold values from -6 to 6
- slopes: float32 [112], P('head'), may hold values from 7.324219e-05 to 0.025
- seg_blocks: int32 [8], replicated, may hold values from 1 to 32, 48 in all
- request_row: int32 [8], replicated, may hold values from 0 to 7, each once
- out_weight: bfloat16 [14336, 14336], P('head', 'seq'), may hold values from -0.046875 to 0.046875
- residual: bfloat16 [2, 8, 14336], P(None, 'head', 'seq'), may hold values from -6 to 6
Outputs:
- mixed: bfloat16 [2, 8, 14336], P(None, 'head', 'seq')
Inputs may be any that keep to these rules, and one draw needn't show every extreme that they name: `seg_blocks`: the requests are packed in order from block 0; 48 blocks are used and the rest of the cache is unused. `request_row`: each query row belongs to exactly one request.
All inputs are finite; a program needn't handle non-finite values.
Results may differ from a plain program's by a relative error of at most 0.006.
Values may be sent and summed in bfloat16 or wider, within the bound.
A program may use at most 64 MiB of HBM per device.

v0:
```python
import math
import jax
import jax.numpy as jnp
from jax import lax
from jax.sharding import PartitionSpec as P

BLK = 128
NEG = -1e30


def combine(first, second):
    top_a, sum_a, acc_a = first
    top_b, sum_b, acc_b = second
    top = jnp.maximum(top_a, top_b)
    weight_a = jnp.exp(top_a - top)
    weight_b = jnp.exp(top_b - top)
    return (
        top,
        sum_a * weight_a + sum_b * weight_b,
        acc_a * weight_a[..., None] + acc_b * weight_b[..., None],
    )


def self_terms(query, key_new, value_new, slopes, scale):
    query = query.astype(jnp.float32)
    key_new = key_new.astype(jnp.float32)
    value_new = value_new.astype(jnp.float32)
    first = jnp.sum(query[0] * key_new[0], axis=-1) * scale
    cross = jnp.sum(query[1] * key_new[0], axis=-1) * scale - slopes
    second = jnp.sum(query[1] * key_new[1], axis=-1) * scale
    upper = jnp.maximum(cross, second)
    e_cross = jnp.exp(cross - upper)
    e_second = jnp.exp(second - upper)
    top = jnp.stack([first, upper])
    total = jnp.stack([jnp.ones_like(first), e_cross + e_second])
    acc = jnp.stack(
        [value_new[0], e_cross[..., None] * value_new[0] + e_second[..., None] * value_new[1]]
    )
    return (top, total, acc)


def body(
    queries,
    new_keys,
    new_values,
    cache_keys,
    cache_values,
    slopes,
    seg_blocks,
    request_row,
    out_weight,
    residual,
):
    heads = slopes.shape[0]
    width = queries.shape[2]
    hdim = width // heads
    requests = seg_blocks.shape[0]
    own_rows = queries.shape[1]
    blocks = cache_keys.shape[0] // BLK
    scale = 1.0 / math.sqrt(hdim)
    everyone = lax.all_gather(queries, "seq", axis=1, tiled=True)
    place = lax.axis_index("seq")
    starts = jnp.cumsum(seg_blocks) - seg_blocks
    index = place * blocks + jnp.arange(blocks, dtype=jnp.int32)
    hit = (index[:, None] >= starts[None, :]) & (index[:, None] < (starts + seg_blocks)[None, :])
    live = jnp.any(hit, axis=1)
    block_row = jnp.sum(jnp.where(hit, request_row[None, :], 0), axis=1)
    first = jnp.sum(jnp.where(hit, starts[None, :], 0), axis=1)
    length = jnp.sum(jnp.where(hit, seg_blocks[None, :], 0), axis=1)
    base = length * BLK - (index - first) * BLK
    block_query = jnp.take(everyone, block_row, axis=1).reshape(2, blocks, heads, hdim)
    keys = cache_keys.reshape(blocks, BLK, heads, hdim)
    values = cache_values.reshape(blocks, BLK, heads, hdim)
    scores = (
        jnp.einsum("sbhd,bthd->bsht", block_query, keys, preferred_element_type=jnp.float32) * scale
    )
    dist = (
        base[:, None, None]
        + jnp.arange(2, dtype=jnp.int32)[None, :, None]
        - jnp.arange(BLK, dtype=jnp.int32)[None, None, :]
    ).astype(jnp.float32)
    scores = scores - slopes[None, None, :, None] * dist[:, :, None, :]
    top = jnp.max(scores, axis=-1)
    probs = jnp.exp(scores - top[..., None])
    total = jnp.sum(probs, axis=-1)
    acc = jnp.einsum(
        "bsht,bthd->bshd", probs.astype(jnp.bfloat16), values, preferred_element_type=jnp.float32
    )
    top = jnp.where(live[:, None, None], top, NEG)
    total = jnp.where(live[:, None, None], total, 0.0)
    acc = jnp.where(live[:, None, None, None], acc, 0.0)
    rowhot = (block_row[:, None] == jnp.arange(requests, dtype=jnp.int32)[None, :]) & live[:, None]
    tab_top = jnp.max(jnp.where(rowhot[:, :, None, None], top[:, None], NEG), axis=0).transpose(
        1, 0, 2
    )
    ratio = jnp.exp(top - jnp.take(tab_top, block_row, axis=1).transpose(1, 0, 2))
    onehot = rowhot.astype(jnp.float32)
    tab_sum = jnp.einsum("br,bsh->srh", onehot, ratio * total, precision=lax.Precision.HIGHEST)
    tab_acc = jnp.einsum(
        "br,bshd->srhd", onehot, ratio[..., None] * acc, precision=lax.Precision.HIGHEST
    )
    mine = self_terms(
        queries.reshape(2, own_rows, heads, hdim),
        new_keys.reshape(2, own_rows, heads, hdim),
        new_values.reshape(2, own_rows, heads, hdim),
        slopes,
        scale,
    )
    got_top, got_sum, got_acc = (
        lax.all_to_all(tab_top[None], "seq", split_axis=2, concat_axis=0, tiled=True),
        lax.all_to_all(tab_sum[None], "seq", split_axis=2, concat_axis=0, tiled=True),
        lax.all_to_all(tab_acc[None], "seq", split_axis=2, concat_axis=0, tiled=True),
    )
    highest = jnp.max(got_top, axis=0)
    factor = jnp.exp(got_top - highest[None])
    gathered_sum = jnp.sum(got_sum * factor, axis=0)
    gathered_acc = jnp.sum(got_acc * factor[..., None], axis=0)
    top_own, sum_own, acc_own = combine((highest, gathered_sum, gathered_acc), mine)
    attended = (acc_own / sum_own[..., None]).astype(jnp.bfloat16).reshape(2, own_rows, width)
    projected = jnp.einsum(
        "srx,xy->sry",
        lax.all_gather(attended, "seq", axis=1, tiled=True),
        out_weight,
        preferred_element_type=jnp.float32,
    )
    summed = lax.psum_scatter(
        projected.astype(jnp.bfloat16), "head", scatter_dimension=1, tiled=True
    ).astype(jnp.float32)
    return (residual.astype(jnp.float32) + summed).astype(jnp.bfloat16)


def solution(mesh):
    in_specs = (
        P(None, "seq", "head"),
        P(None, "seq", "head"),
        P(None, "seq", "head"),
        P("seq", "head"),
        P("seq", "head"),
        P("head"),
        P(),
        P(),
        P("head", "seq"),
        P(None, "head", "seq"),
    )
    out_specs = P(None, "head", "seq")
    return jax.shard_map(body, mesh=mesh, in_specs=in_specs, out_specs=out_specs, check_vma=False)
```

profile of v0, /device:TPU:0, one launch (start us, length us, event | category | flops | bytes accessed | tf_op | source)
XLA Modules:
  0.0 161.4 jit_solution(8189962348176017590)
XLA Ops:
  0.0 0.8 reduce-window.8
  0.8 0.7 iota_add_fusion.1
  1.5 0.9 select_reduce_fusion.2
  2.6 32.6 %all_gather.6 = bf16[2,8,3584]{2,0,1:T(2,128)(2,1)S(1)} all-gather(bf16[2,1,3584]{2,0,1:T(2,128)(2,1)} %param.10), channel_id=1, replica_groups=mesh['seq'=8,'head'=4] {'seq'}, dimensions={1}, use_global_device_ids=true | all-gather | bytes 129024 | tf_op jit(solution)/shard_map/all_gather | solution.py:61
  35.4 12.9 %reshape.655 = bf16[8,128,28,128]{3,2,1,0:T(8,128)(2,1)} reshape(bf16[1024,3584]{1,0:T(8,128)(2,1)} %param.13) | data formatting | bytes 14680064 | tf_op jit(solution)/shard_map/reshape | solution.py:72
  48.3 0.8 gather_fusion
  49.2 7.4 %fusion.67 = (f32[8,2,28]{1,2,0:T(8,128)S(1)}, f32[8,2,28,128]{3,1,2,0:T(2,128)S(1)}) fusion(f32[8,2,128]{2,1,0:T(2,128)S(1)} %subtract_convert_fusion, f32[28]{0:T(128)S(1)} %copy-done.4, bf16[8,128,28,128]{3,2,1,0:T(8,128)(2,1)} %reshape.655, bf16[2,8,28,128]{3,1,2,0:T(8,128)(2,1)S(1)} %bitcast_select_fusion), kind=kOutput, calls=%fused_computation.103 | convolution fusion | flops 14908992 | bytes 7694192 | tf_op jit(solution)/shard_map/sbhd,bthd->bsht/dot_general | solution.py:75
  56.9 0.6 copy.210
  57.5 5.5 %all-to-all-start.1 = ((f32[1,2,8,28]{3,1,0,2:T(2,128)}), f32[1,2,8,28]{3,1,0,2:T(2,128)S(1)}, u32[]{:S(2)}, u32[]{:S(2)}) async-start(f32[1,2,8,28]{3,1,0,2:T(2,128)} %bitcast.107.clone.2), calls=%async_computation.1 | async-start | bytes 16384 | tf_op jit(solution)/shard_map/all_to_all | solution.py:110
  63.0 1.3 gather_fusion.1
  64.5 12.9 %reshape.656 = bf16[8,128,28,128]{3,2,1,0:T(8,128)(2,1)} reshape(bf16[1024,3584]{1,0:T(8,128)(2,1)} %param.14) | data formatting | bytes 14680064 | tf_op jit(solution)/shard_map/reshape | solution.py:73
  77.4 0.6 fusion.29
  78.0 6.6 %fusion.24 = f32[8,2,28,128]{3,1,2,0:T(2,128)S(1)} fusion(bf16[8,128,28,128]{3,2,1,0:T(8,128)(2,1)} %reshape.656, pred[8]{0:T(512)(128)(4,1)S(1)} %fusion.66, f32[8,2,28,128]{3,1,2,0:T(2,128)S(1)} %get-tuple-element.24, f32[8,2,28]{1,2,0:T(8,128)S(1)} %get-tuple-element.23, f32[8,2,28]{1,2,0:T(8,128)S(1)} %copy.154), kind=kOutput, calls=%fused_computation.16 | convolution fusion | flops 14909440 | bytes 7802376 | tf_op jit(solution)/shard_map/bsht,bthd->bshd/dot_general | solution.py:86
  85.8 0.9 copy.158
  86.7 0.6 copy.164
  87.3 0.6 dynamic-slice
  88.6 6.0 %all-to-all-start.2 = ((f32[1,2,8,28]{3,1,0,2:T(2,128)}), f32[1,2,8,28]{3,1,0,2:T(2,128)S(1)}, u32[]{:S(2)}, u32[]{:S(2)}) async-start(f32[1,2,8,28]{3,1,0,2:T(2,128)} %copy.164), calls=%async_computation.2 | async-start | bytes 16384 | tf_op jit(solution)/shard_map/all_to_all | solution.py:111
  94.8 6.4 %all-to-all-done.2 = f32[1,2,8,28]{3,1,0,2:T(2,128)S(1)} async-done(((f32[1,2,8,28]{3,1,0,2:T(2,128)}), f32[1,2,8,28]{3,1,0,2:T(2,128)S(1)}, u32[]{:S(2)}, u32[]{:S(2)}) %all-to-all-start.2) | async-done | bytes 1824 | tf_op jit(solution)/shard_map/all_to_all | solution.py:111
  101.2 3.4 %all-to-all-start = ((f32[1,2,8,28,128]{4,1,3,0,2:T(2,128)}), f32[1,2,8,28,128]{4,1,3,0,2:T(2,128)S(1)}, u32[]{:S(2)}, u32[]{:S(2)}) async-start(f32[1,2,8,28,128]{4,1,3,0,2:T(2,128)} %copy.158), calls=%async_computation | async-start | bytes 458752 | tf_op jit(solution)/shard_map/all_to_all | solution.py:112
  105.0 7.7 %all-to-all-done = f32[1,2,8,28,128]{4,1,3,0,2:T(2,128)S(1)} async-done(((f32[1,2,8,28,128]{4,1,3,0,2:T(2,128)}), f32[1,2,8,28,128]{4,1,3,0,2:T(2,128)S(1)}, u32[]{:S(2)}, u32[]{:S(2)}) %all-to-all-start) | async-done | bytes 229408 | tf_op jit(solution)/shard_map/all_to_all | solution.py:112
  113.1 30.6 %all_gather.7 = bf16[2,8,3584]{2,0,1:T(2,128)(2,1)S(1)} all-gather(bf16[2,1,3584]{2,0,1:T(2,128)(2,1)S(1)} %fusion.37), channel_id=1, replica_groups=mesh['seq'=8,'head'=4] {'seq'}, dimensions={1}, use_global_device_ids=true | all-gather | bytes 129024 | tf_op jit(solution)/shard_map/all_gather | solution.py:122
  143.6 6.4 %fusion.6 = bf16[2,8,1792]{2,1,0:T(8,128)(2,1)S(1)} fusion(bf16[3584,1792]{1,0:T(8,128)(2,1)} %param.18, bf16[2,8,3584]{2,0,1:T(2,128)(2,1)S(1)} %all_gather.7), kind=kOutput, calls=%fused_computation.8 | convolution fusion | flops 205549568 | bytes 13017088 | tf_op jit(solution)/shard_map/srx,xy->sry/dot_general | solution.py:120
  150.1 10.7 %all-reduce.1 = bf16[2,8,1792]{2,1,0:T(8,128)(2,1)S(1)} all-reduce(bf16[2,8,1792]{2,1,0:T(8,128)(2,1)S(1)} %fusion.6), channel_id=2, replica_groups=mesh['seq'=8,'head'=4] {'head'}, use_global_device_ids=true, to_apply=%region_14.15.clone | all-reduce | flops 28672 | bytes 114688
  160.8 0.6 add_convert_fusion
  (57 shorter events, 3.2 us)
Async XLA Ops:
  0.0 49.1 %copy-start.4 = (f32[28]{0:T(128)S(1)}, f32[28]{0:T(128)}, u32[]{:S(2)}) copy-start(f32[28]{0:T(128)} %param.15) | copy-start | bytes 340
  48.3 14.7 %copy-start.1 = (bf16[2,1,3584]{2,0,1:T(2,128)(2,1)S(1)}, bf16[2,1,3584]{2,0,1:T(2,128)(2,1)}, u32[]{:S(2)}) copy-start(bf16[2,1,3584]{2,0,1:T(2,128)(2,1)} %param.10) | copy-start | bytes 43012
  57.5 31.0 %all-to-all-start.1 = ((f32[1,2,8,28]{3,1,0,2:T(2,128)}), f32[1,2,8,28]{3,1,0,2:T(2,128)S(1)}, u32[]{:S(2)}, u32[]{:S(2)}) async-start(f32[1,2,8,28]{3,1,0,2:T(2,128)} %bitcast.107.clone.2), calls=%async_computation.1 | async-start | bytes 16384 | tf_op jit(solution)/shard_map/all_to_all | solution.py:110
  77.4 7.6 %copy-start.2 = (bf16[2,1,3584]{2,0,1:T(2,128)(2,1)S(1)}, bf16[2,1,3584]{2,0,1:T(2,128)(2,1)}, u32[]{:S(2)}) copy-start(bf16[2,1,3584]{2,0,1:T(2,128)(2,1)} %param.11) | copy-start | bytes 43012
  77.4 7.8 %copy-start = (bf16[2,1,3584]{2,0,1:T(2,128)(2,1)S(1)}, bf16[2,1,3584]{2,0,1:T(2,128)(2,1)}, u32[]{:S(2)}) copy-start(bf16[2,1,3584]{2,0,1:T(2,128)(2,1)} %param.12) | copy-start | bytes 43012
  77.4 9.9 %copy-start.5 = (u32[32]{0:T(128)S(1)}, u32[32]{0:T(128)}, u32[]{:S(2)}) copy-start(u32[32]{0:T(128)} %constant.63) | copy-start | bytes 388
  88.6 12.6 %all-to-all-start.2 = ((f32[1,2,8,28]{3,1,0,2:T(2,128)}), f32[1,2,8,28]{3,1,0,2:T(2,128)S(1)}, u32[]{:S(2)}, u32[]{:S(2)}) async-start(f32[1,2,8,28]{3,1,0,2:T(2,128)} %copy.164), calls=%async_computation.2 | async-start | bytes 16384 | tf_op jit(solution)/shard_map/all_to_all | solution.py:111
  94.8 66.0 %copy-start.3 = (bf16[2,2,1792]{2,1,0:T(2,128)(2,1)S(1)}, bf16[2,2,1792]{2,1,0:T(2,128)(2,1)}, u32[]{:S(2)}) copy-start(bf16[2,2,1792]{2,1,0:T(2,128)(2,1)} %param.19) | copy-start | bytes 43012
  101.2 11.4 %all-to-all-start = ((f32[1,2,8,28,128]{4,1,3,0,2:T(2,128)}), f32[1,2,8,28,128]{4,1,3,0,2:T(2,128)S(1)}, u32[]{:S(2)}, u32[]{:S(2)}) async-start(f32[1,2,8,28,128]{4,1,3,0,2:T(2,128)} %copy.158), calls=%async_computation | async-start | bytes 458752 | tf_op jit(solution)/shard_map/all_to_all | solution.py:112
where the time goes:
time: 163 us; the launch traced here: 161 us
  blocking collectives  73.9 us (45%)
  local copies, waits for them, and re-layouts  31.6 us (19%)
  matrix products  20.8 us (13%)
  starting transfers between devices  14.9 us (9%)
  waiting for transfers between devices  14.1 us (9%)
  other arithmetic  5.31 us (3%)
    all_gather x1, blocking collectives, body(): everyone = lax.all_gather(queries, 'seq', axis=1, tiled=True)  32.6 us
    all_gather x1, blocking collectives, body(): lax.all_gather(attended, 'seq', axis=1, tiled=True)  30.6 us
    reshape x1, local copies, waits for them, and re-layouts, body(): values = cache_values.reshape(blocks, BLK, heads, hdim)  12.9 us
    reshape x1, local copies, waits for them, and re-layouts, body(): keys = cache_keys.reshape(blocks, BLK, heads, hdim)  12.9 us
    unnamed x1, blocking collectives  10.7 us
    all_to_all x1, waiting for transfers between devices, body(): lax.all_to_all(tab_acc[None], 'seq', split_axis=2, concat_axis=0, tiled=T...  7.65 us
    dot_general x1, matrix products, body(): jnp.einsum('sbhd,bthd->bsht', block_query, keys, preferred_element_type=j...  7.37 us
    dot_general x1, matrix products, body(): jnp.einsum('bsht,bthd->bshd', probs.astype(jnp.bfloat16), values, preferr...  6.58 us
  transfers between devices with their start and end apart: 3, of which 2 were waited for; matrix products, arithmetic and copies ran while one was open for 16% of the time, Pallas kernels for 0%

commit v1 on v0

--- a/solution.py
+++ b/solution.py
@@ -6,6 +6,32 @@
 
 BLK = 128
 NEG = -1e30
+
+
+def do_the_corner(obj, row_dim):
+    obj = jnp.moveaxis(obj, 0, row_dim)
+    step_out = obj.shape
+    return obj.reshape(
+        *step_out[:row_dim], step_out[row_dim] * step_out[row_dim + 1], *step_out[row_dim + 2 :]
+    )
+
+
+def take_samples(tile_in, named_axis):
+    nd = lax.axis_size(named_axis)
+    block_last = tile_in[None]
+    for dev_i in range(nd.bit_length() - 1):
+        x_next = 1 << dev_i
+        local_next = lax.ppermute(
+            block_last, named_axis, list(map(lambda num: (num, num ^ x_next), range(nd)))
+        )
+        e_next = jnp.stack([block_last, local_next])
+        outcome_arr = lax.axis_index(named_axis) >> dev_i & 1
+        block_last = jnp.where(outcome_arr == 0, e_next, e_next[::-1]).reshape(-1, *tile_in.shape)
+    return block_last
+
+
+def arrange_counts_all(a0, s0, d0):
+    return do_the_corner(take_samples(a0, s0), d0)
 
 
 def combine(first, second):
@@ -119,7 +145,7 @@
     attended = (acc_own / sum_own[..., None]).astype(jnp.bfloat16).reshape(2, own_rows, width)
     projected = jnp.einsum(
         "srx,xy->sry",
-        lax.all_gather(attended, "seq", axis=1, tiled=True),
+        arrange_counts_all(attended, "seq", 1),
         out_weight,
         preferred_element_type=jnp.float32,
     )

time: 163 us -> 144 us (0.88)
  blocking collectives: 73.9 us -> 43.3 us
  waiting for transfers between devices: 14.1 us -> 24.7 us
    all_gather x1 -> x0, blocking collectives: 30.6 us -> none  [body(): lax.all_gather(attended, 'seq', axis=1, tiled=True)]
    ppermute x0 -> x3, waiting for transfers between devices: none -> 11 us  [take_samples(): lax.ppermute(block_last, named_axis, list(map(lambda num: (num, num ^ x_n...]
  transfers between devices with their start and end apart: 3 -> 6, of which waited for: 2 -> 5; matrix products, arithmetic and copies ran while one was open for 16% -> 18% of each run, Pallas kernels for 0% -> 0%
where the time goes in v1:
time: 144 us; the launch traced here: 143 us
  blocking collectives  43.3 us (30%)
  local copies, waits for them, and re-layouts  31.6 us (22%)
  waiting for transfers between devices  24.7 us (17%)
  matrix products  20.8 us (14%)
  starting transfers between devices  15.6 us (11%)
  other arithmetic  5.88 us (4%)
    all_gather x1, blocking collectives, body(): everyone = lax.all_gather(queries, 'seq', axis=1, tiled=True)  32.6 us
    reshape x1, local copies, waits for them, and re-layouts, body(): values = cache_values.reshape(blocks, BLK, heads, hdim)  12.9 us
    reshape x1, local copies, waits for them, and re-layouts, body(): keys = cache_keys.reshape(blocks, BLK, heads, hdim)  12.9 us
    ppermute x3, waiting for transfers between devices, take_samples(): lax.ppermute(block_last, named_axis, list(map(lambda num: (num, num ^ x_n...  11 us
    unnamed x1, blocking collectives  10.7 us
    dot_general x1, matrix products, body(): jnp.einsum('sbhd,bthd->bsht', block_query, keys, preferred_element_type=j...  7.37 us
    all_to_all x1, waiting for transfers between devices, body(): lax.all_to_all(tab_acc[None], 'seq', split_axis=2, concat_axis=0, tiled=T...  7.16 us
    all_to_all x1, waiting for transfers between devices, body(): lax.all_to_all(tab_sum[None], 'seq', split_axis=2, concat_axis=0, tiled=T...  6.58 us
  transfers between devices with their start and end apart: 6, of which 5 were waited for; matrix products, arithmetic and copies ran while one was open for 18% of the time, Pallas kernels for 0%

profile of v1, /device:TPU:0, one launch (start us, length us, event | category | flops | bytes accessed | tf_op | source)
XLA Modules:
  0.0 142.9 jit_solution(15047358756827978884)
XLA Ops:
  0.0 0.8 reduce-window.8
  0.8 0.7 iota_add_fusion.1
  1.5 0.9 select_reduce_fusion.2
  2.6 32.6 %all_gather.3 = bf16[2,8,3584]{2,0,1:T(2,128)(2,1)S(1)} all-gather(bf16[2,1,3584]{2,0,1:T(2,128)(2,1)} %param.10), channel_id=1, replica_groups=mesh['seq'=8,'head'=4] {'seq'}, dimensions={1}, use_global_device_ids=true | all-gather | bytes 129024 | tf_op jit(solution)/shard_map/all_gather | solution.py:87
  35.4 12.9 %reshape.748 = bf16[8,128,28,128]{3,2,1,0:T(8,128)(2,1)} reshape(bf16[1024,3584]{1,0:T(8,128)(2,1)} %param.13) | data formatting | bytes 14680064 | tf_op jit(solution)/shard_map/reshape | solution.py:98
  48.3 0.8 gather_fusion
  49.2 7.4 %fusion.73 = (f32[8,2,28]{1,2,0:T(8,128)S(1)}, f32[8,2,28,128]{3,1,2,0:T(2,128)S(1)}) fusion(f32[8,2,128]{2,1,0:T(2,128)S(1)} %subtract_convert_fusion, f32[28]{0:T(128)S(1)} %copy-done.4, bf16[8,128,28,128]{3,2,1,0:T(8,128)(2,1)} %reshape.748, bf16[2,8,28,128]{3,1,2,0:T(8,128)(2,1)S(1)} %bitcast_select_fusion), kind=kOutput, calls=%fused_computation.118 | convolution fusion | flops 14908992 | bytes 7694192 | tf_op jit(solution)/shard_map/sbhd,bthd->bsht/dot_general | solution.py:101
  56.9 0.6 copy.218
  57.5 5.5 %all-to-all-start.1 = ((f32[1,2,8,28]{3,1,0,2:T(2,128)}), f32[1,2,8,28]{3,1,0,2:T(2,128)S(1)}, u32[]{:S(2)}, u32[]{:S(2)}) async-start(f32[1,2,8,28]{3,1,0,2:T(2,128)} %bitcast.127.clone.2), calls=%async_computation.1 | async-start | bytes 16384 | tf_op jit(solution)/shard_map/all_to_all | solution.py:136
  63.0 1.3 gather_fusion.1
  64.5 12.9 %reshape.749 = bf16[8,128,28,128]{3,2,1,0:T(8,128)(2,1)} reshape(bf16[1024,3584]{1,0:T(8,128)(2,1)} %param.14) | data formatting | bytes 14680064 | tf_op jit(solution)/shard_map/reshape | solution.py:99
  78.0 6.6 %fusion.24 = f32[8,2,28,128]{3,1,2,0:T(2,128)S(1)} fusion(bf16[8,128,28,128]{3,2,1,0:T(8,128)(2,1)} %reshape.749, pred[8]{0:T(512)(128)(4,1)S(1)} %fusion.72, f32[8,2,28,128]{3,1,2,0:T(2,128)S(1)} %get-tuple-element.30, f32[8,2,28]{1,2,0:T(8,128)S(1)} %get-tuple-element.29, f32[8,2,28]{1,2,0:T(8,128)S(1)} %copy.158), kind=kOutput, calls=%fused_computation.16 | convolution fusion | flops 14909440 | bytes 7802376 | tf_op jit(solution)/shard_map/bsht,bthd->bshd/dot_general | solution.py:112
  85.8 0.9 copy.162
  86.7 0.6 copy.168
  87.3 6.0 %all-to-all-start.2 = ((f32[1,2,8,28]{3,1,0,2:T(2,128)}), f32[1,2,8,28]{3,1,0,2:T(2,128)S(1)}, u32[]{:S(2)}, u32[]{:S(2)}) async-start(f32[1,2,8,28]{3,1,0,2:T(2,128)} %copy.168), calls=%async_computation.2 | async-start | bytes 16384 | tf_op jit(solution)/shard_map/all_to_all | solution.py:137
  93.3 6.6 %all-to-all-done.2 = f32[1,2,8,28]{3,1,0,2:T(2,128)S(1)} async-done(((f32[1,2,8,28]{3,1,0,2:T(2,128)}), f32[1,2,8,28]{3,1,0,2:T(2,128)S(1)}, u32[]{:S(2)}, u32[]{:S(2)}) %all-to-all-start.2) | async-done | bytes 1824 | tf_op jit(solution)/shard_map/all_to_all | solution.py:137
  99.9 3.6 %all-to-all-start = ((f32[1,2,8,28,128]{4,1,3,0,2:T(2,128)}), f32[1,2,8,28,128]{4,1,3,0,2:T(2,128)S(1)}, u32[]{:S(2)}, u32[]{:S(2)}) async-start(f32[1,2,8,28,128]{4,1,3,0,2:T(2,128)} %copy.162), calls=%async_computation | async-start | bytes 458752 | tf_op jit(solution)/shard_map/all_to_all | solution.py:138
  104.1 7.2 %all-to-all-done = f32[1,2,8,28,128]{4,1,3,0,2:T(2,128)S(1)} async-done(((f32[1,2,8,28,128]{4,1,3,0,2:T(2,128)}), f32[1,2,8,28,128]{4,1,3,0,2:T(2,128)S(1)}, u32[]{:S(2)}, u32[]{:S(2)}) %all-to-all-start) | async-done | bytes 229408 | tf_op jit(solution)/shard_map/all_to_all | solution.py:138
  111.9 3.6 %collective-permute-done = bf16[1,2,1,3584]{3,1,2,0:T(2,128)(2,1)S(1)} collective-permute-done((bf16[1,2,1,3584]{3,1,2,0:T(2,128)(2,1)S(1)}, bf16[1,2,1,3584]{3,1,2,0:T(2,128)(2,1)S(1)}, u32[]{:S(2)}, u32[]{:S(2)}) %collective-permute-start) | collective-permute-done | bytes 14368 | tf_op jit(solution)/shard_map/ppermute | solution.py:24
  115.7 3.9 %collective-permute-done.1 = bf16[2,2,1,3584]{3,1,0,2:T(2,128)(2,1)S(1)} collective-permute-done((bf16[2,2,1,3584]{3,1,0,2:T(2,128)(2,1)S(1)}, bf16[2,2,1,3584]{3,1,0,2:T(2,128)(2,1)S(1)}, u32[]{:S(2)}, u32[]{:S(2)}) %collective-permute-start.1) | collective-permute-done | bytes 28704 | tf_op jit(solution)/shard_map/ppermute | solution.py:24
  121.4 3.5 %collective-permute-done.2 = bf16[4,2,1,3584]{3,1,0,2:T(2,128)(2,1)S(1)} collective-permute-done((bf16[4,2,1,3584]{3,1,0,2:T(2,128)(2,1)S(1)}, bf16[4,2,1,3584]{3,1,0,2:T(2,128)(2,1)S(1)}, u32[]{:S(2)}, u32[]{:S(2)}) %collective-permute-start.2) | collective-permute-done | bytes 57376 | tf_op jit(solution)/shard_map/ppermute | solution.py:24
  125.1 6.4 %fusion.6 = bf16[2,8,1792]{2,1,0:T(8,128)(2,1)S(1)} fusion(bf16[3584,1792]{1,0:T(8,128)(2,1)} %param.18, bf16[8,2,1,3584]{3,1,0,2:T(2,128)(2,1)S(1)} %bitcast.151), kind=kOutput, calls=%fused_computation.8 | convolution fusion | flops 205549568 | bytes 13017088 | tf_op jit(solution)/shard_map/srx,xy->sry/dot_general | solution.py:146
  131.5 10.7 %all-reduce.1 = bf16[2,8,1792]{2,1,0:T(8,128)(2,1)S(1)} all-reduce(bf16[2,8,1792]{2,1,0:T(8,128)(2,1)S(1)} %fusion.6), channel_id=2, replica_groups=mesh['seq'=8,'head'=4] {'head'}, use_global_device_ids=true, to_apply=%region_14.15.clone | all-reduce | flops 28672 | bytes 114688
  142.3 0.6 add_convert_fusion
  (71 shorter events, 5.6 us)
Async XLA Ops:
  0.0 49.1 %copy-start.4 = (f32[28]{0:T(128)S(1)}, f32[28]{0:T(128)}, u32[]{:S(2)}) copy-start(f32[28]{0:T(128)} %param.15) | copy-start | bytes 340
  48.3 14.7 %copy-start = (bf16[2,1,3584]{2,0,1:T(2,128)(2,1)S(1)}, bf16[2,1,3584]{2,0,1:T(2,128)(2,1)}, u32[]{:S(2)}) copy-start(bf16[2,1,3584]{2,0,1:T(2,128)(2,1)} %param.10) | copy-start | bytes 43012
  57.5 29.8 %all-to-all-start.1 = ((f32[1,2,8,28]{3,1,0,2:T(2,128)}), f32[1,2,8,28]{3,1,0,2:T(2,128)S(1)}, u32[]{:S(2)}, u32[]{:S(2)}) async-start(f32[1,2,8,28]{3,1,0,2:T(2,128)} %bitcast.127.clone.2), calls=%async_computation.1 | async-start | bytes 16384 | tf_op jit(solution)/shard_map/all_to_all | solution.py:136
  77.4 7.6 %copy-start.1 = (bf16[2,1,3584]{2,0,1:T(2,128)(2,1)S(1)}, bf16[2,1,3584]{2,0,1:T(2,128)(2,1)}, u32[]{:S(2)}) copy-start(bf16[2,1,3584]{2,0,1:T(2,128)(2,1)} %param.11) | copy-start | bytes 43012
  77.4 7.8 %copy-start.2 = (bf16[2,1,3584]{2,0,1:T(2,128)(2,1)S(1)}, bf16[2,1,3584]{2,0,1:T(2,128)(2,1)}, u32[]{:S(2)}) copy-start(bf16[2,1,3584]{2,0,1:T(2,128)(2,1)} %param.12) | copy-start | bytes 43012
  77.4 42.7 %copy-start.5 = (u32[32]{0:T(128)S(1)}, u32[32]{0:T(128)}, u32[]{:S(2)}) copy-start(u32[32]{0:T(128)} %constant.67) | copy-start | bytes 388
  87.3 12.6 %all-to-all-start.2 = ((f32[1,2,8,28]{3,1,0,2:T(2,128)}), f32[1,2,8,28]{3,1,0,2:T(2,128)S(1)}, u32[]{:S(2)}, u32[]{:S(2)}) async-start(f32[1,2,8,28]{3,1,0,2:T(2,128)} %copy.168), calls=%async_computation.2 | async-start | bytes 16384 | tf_op jit(solution)/shard_map/all_to_all | solution.py:137
  99.9 11.3 %all-to-all-start = ((f32[1,2,8,28,128]{4,1,3,0,2:T(2,128)}), f32[1,2,8,28,128]{4,1,3,0,2:T(2,128)S(1)}, u32[]{:S(2)}, u32[]{:S(2)}) async-start(f32[1,2,8,28,128]{4,1,3,0,2:T(2,128)} %copy.162), calls=%async_computation | async-start | bytes 458752 | tf_op jit(solution)/shard_map/all_to_all | solution.py:138
  111.6 30.7 %copy-start.3 = (bf16[2,2,1792]{2,1,0:T(2,128)(2,1)S(1)}, bf16[2,2,1792]{2,1,0:T(2,128)(2,1)}, u32[]{:S(2)}) copy-start(bf16[2,2,1792]{2,1,0:T(2,128)(2,1)} %param.19) | copy-start | bytes 43012
  111.7 3.8 %collective-permute-start = (bf16[1,2,1,3584]{3,1,2,0:T(2,128)(2,1)S(1)}, bf16[1,2,1,3584]{3,1,2,0:T(2,128)(2,1)S(1)}, u32[]{:S(2)}, u32[]{:S(2)}) collective-permute-start(bf16[1,2,1,3584]{3,1,2,0:T(2,128)(2,1)S(1)} %fusion.40), channel_id=1, source_target_pairs={{0,4},{4,0},{8,12},{12,8},{16,20},{20,16},{24,28},{28,24},{1,5},{5... | collective-permute-start | bytes 43016 | tf_op jit(solution)/shard_map/ppermute | solution.py:24
  115.6 3.9 %collective-permute-start.1 = (bf16[2,2,1,3584]{3,1,0,2:T(2,128)(2,1)S(1)}, bf16[2,2,1,3584]{3,1,0,2:T(2,128)(2,1)S(1)}, u32[]{:S(2)}, u32[]{:S(2)}) collective-permute-start(bf16[2,2,1,3584]{3,1,0,2:T(2,128)(2,1)S(1)} %get-tuple-element.18), channel_id=1, source_target_pairs={{0,8},{4,12},{8,0},{12,4},{16,24},{20,28},{24,16},{28,20},{1,9},{5... | collective-permute-start | bytes 86024 | tf_op jit(solution)/shard_map/ppermute | solution.py:24
  119.7 5.2 %collective-permute-start.2 = (bf16[4,2,1,3584]{3,1,0,2:T(2,128)(2,1)S(1)}, bf16[4,2,1,3584]{3,1,0,2:T(2,128)(2,1)S(1)}, u32[]{:S(2)}, u32[]{:S(2)}) collective-permute-start(bf16[4,2,1,3584]{3,1,0,2:T(2,128)(2,1)S(1)} %bitcast.153), channel_id=1, source_target_pairs={{0,16},{4,20},{8,24},{12,28},{16,0},{20,4},{24,8},{28,12},{1,17},{... | collective-permute-start | bytes 172040 | tf_op jit(solution)/shard_map/ppermute | solution.py:24
